TPU v7x, 32 devices: a whole 2x2x4 slice. The times are simulated.
32 devices in a mesh: dp: 8 (over y, x, core), hid: 4 (over z).
Axes of the slice: x: 2, y: 2, z: 4, core: 2. Of those that a mesh axis runs over, the one named last changes fastest.
Arguments:
- tokens: bfloat16 [512, 4096], P(('dp', 'hid')), may hold values from -6 to 6
- cotangent: bfloat16 [512, 7680], P('dp', 'hid'), may hold values from -8 to 8
- weights: bfloat16 [2, 7680, 4096], P(None, 'hid'), may hold values from -0.09375 to 0.09375
- basis: bfloat16 [4096, 256], P('dp'), may hold values from -0.09375 to 0.09375
- master: float32 [2, 7680, 4096], P(None, 'hid', 'dp'), may hold values from -0.09375 to 0.09375
- first_moment: float32 [7680, 2, 256], P(('hid', 'dp')), may hold values from -48 to 48
- second_moment: float32 [7680, 2, 256], P(('hid', 'dp')), may hold values from 25 to 2500
Outputs:
- master_new: float32 [2, 7680, 4096], P(None, 'hid', 'dp')
- first_new: float32 [7680, 2, 256], P(('hid', 'dp'))
- second_new: float32 [7680, 2, 256], P(('hid', 'dp'))
All inputs are finite; a program needn't handle non-finite values.
Results may differ from a plain program's by a relative error of at most 0.0003.
Values may be sent and summed in bfloat16 or wider, within the bound.
No kernel may reach another device: no remote copies, remote signals or barrier semaphores. Data moves between devices by JAX's collectives and lax.ppermute only.
A program may use at most 128 MiB of HBM per device.

v0:
```python
import jax
import jax.numpy as jnp
from jax import lax
from jax.sharding import PartitionSpec as P

beta_first = 0.9
beta_second = 0.95
step_size = 0.05
adam_epsilon = 1e-08


def silu_pieces(pre_gate):
    sigmoid_val = jax.nn.sigmoid(pre_gate)
    return (pre_gate * sigmoid_val, sigmoid_val * (1.0 + pre_gate * (1.0 - sigmoid_val)))


def on_device(tokens, cotangent, weights, basis, master, first_moment, second_moment):
    highest = lax.Precision.HIGHEST
    group_tokens = lax.all_gather(tokens, "hid", axis=0, tiled=True)
    projected = jnp.dot(
        group_tokens,
        lax.all_gather(basis, "dp", axis=0, tiled=True),
        preferred_element_type=jnp.float32,
    )
    contract_cols = (((1,), (1,)), ((), ()))
    pre_gate = lax.dot_general(
        group_tokens, weights[0], contract_cols, preferred_element_type=jnp.float32
    )
    pre_up = lax.dot_general(
        group_tokens, weights[1], contract_cols, preferred_element_type=jnp.float32
    )
    activated, silu_slope = silu_pieces(pre_gate)
    upstream = cotangent.astype(jnp.float32)
    grad_gate = upstream * pre_up * silu_slope
    grad_up = upstream * activated
    over_tokens = (((0,), (0,)), ((), ()))
    gate_term = lax.dot_general(
        grad_gate, projected, over_tokens, precision=highest, preferred_element_type=jnp.float32
    )
    up_term = lax.dot_general(
        grad_up, projected, over_tokens, precision=highest, preferred_element_type=jnp.float32
    )
    gradient = lax.psum_scatter(
        jnp.stack([gate_term, up_term], axis=1), "dp", scatter_dimension=0, tiled=True
    )
    first_new = beta_first * first_moment + (1.0 - beta_first) * gradient
    second_new = beta_second * second_moment + (1.0 - beta_second) * gradient * gradient
    direction_share = first_new / (jnp.sqrt(second_new) + adam_epsilon)
    direction = lax.all_gather(direction_share, "dp", axis=0, tiled=True)
    lifted = jnp.einsum("fwr,dr->wfd", direction, basis.astype(jnp.float32), precision=highest)
    master_new = master - step_size * lifted
    return (master_new, first_new, second_new)


def solution(mesh):
    in_specs = (
        P(("dp", "hid"), None),
        P("dp", "hid"),
        P(None, "hid", None),
        P("dp", None),
        P(None, "hid", "dp"),
        P(("hid", "dp"), None, None),
        P(("hid", "dp"), None, None),
    )
    out_specs = (P(None, "hid", "dp"), P(("hid", "dp"), None, None), P(("hid", "dp"), None, None))
    return jax.shard_map(
        on_device, mesh=mesh, in_specs=in_specs, out_specs=out_specs, check_vma=False
    )
```

profile of v0, /device:TPU:0, one launch (start us, length us, event | category | flops | bytes accessed | tf_op | source)
XLA Modules:
  0.0 156.3 jit_solution(17608231928793287839)
XLA Ops:
  7.2 0.0 all-gather.3.cloned.1.call-start
  7.2 0.7 all-gather.3.cloned.1.call-update
  7.9 0.0 reduce-scatter.2.cloned.1.call-start
  7.9 17.6 %all_gather.9 = bf16[64,4096]{1,0:T(8,128)(2,1)S(1)} all-gather(bf16[16,4096]{1,0:T(8,128)(2,1)} %param.7), channel_id=1, replica_groups=mesh['dp'=8,'hid'=4] {'hid'}, dimensions={0}, use_global_device_ids=true | all-gather | bytes 655360 | tf_op jit(solution)/shard_map/all_gather | solution.py:19
  25.5 8.8 %fusion = f32[64,1920]{1,0:T(8,128)S(1)} fusion(bf16[64,4096]{1,0:T(8,128)(2,1)S(1)} %all_gather.9, bf16[2,1920,4096]{2,1,0:T(8,128)(2,1)} %param.9), kind=kOutput, calls=%fused_computation | convolution fusion | flops 1006632960 | bytes 16744448 | tf_op jit(solution)/shard_map/dot_general | solution.py:26
  34.3 0.0 copy-done.3
  34.3 8.8 %fusion.9 = f32[64,1920]{1,0:T(8,128)S(1)} fusion(bf16[64,4096]{1,0:T(8,128)(2,1)S(1)} %all_gather.9, bf16[2,1920,4096]{2,1,0:T(8,128)(2,1)} %param.9, bf16[64,1920]{1,0:T(8,128)(2,1)S(1)} %copy-done.3, f32[64,1920]{1,0:T(8,128)S(1)} %fusion), kind=kOutput, calls=%fused_computation.11 | convolution fusion | flops 1007861760 | bytes 17481728 | tf_op jit(solution)/shard_map/dot_general | solution.py:29
  43.2 0.0 all-gather.3.cloned.1.call-done
  43.2 2.0 %fusion.20 = f32[64,256]{1,0:T(8,128)S(1)} fusion(bf16[64,4096]{1,0:T(8,128)(2,1)S(1)} %all_gather.9, bf16[4096,256]{1,0:T(8,128)(2,1)} %all-gather.3.cloned.1.call-done), kind=kOutput, calls=%fused_computation.24 | convolution fusion | flops 134217728 | bytes 2686976 | tf_op jit(solution)/shard_map/dot_general | solution.py:20
  45.3 1.8 %convolution_bitcast_fusion = f32[1920,1,256]{2,0,1:T(8,128)S(1)} fusion(f32[64,256]{1,0:T(8,128)S(1)} %fusion.20, bf16[64,1920]{1,0:T(8,128)(2,1)S(1)} %copy-done.3, f32[64,1920]{1,0:T(8,128)S(1)} %fusion), kind=kOutput, calls=%fused_computation.8 | convolution fusion | flops 378224640 | bytes 2768896 | tf_op jit(solution)/shard_map/dot_general | solution.py:40
  47.0 1.8 %convolution_bitcast_fusion.1 = f32[1920,1,256]{2,0,1:T(8,128)S(1)} fusion(f32[64,1920]{1,0:T(8,128)S(1)} %fusion.9, f32[64,256]{1,0:T(8,128)S(1)} %fusion.20), kind=kOutput, calls=%fused_computation.9 | convolution fusion | flops 377487360 | bytes 2523136 | tf_op jit(solution)/shard_map/dot_general | solution.py:37
  48.8 2.2 %pad_maximum_fusion = f32[1920,2,256]{2,0,1:T(8,128)} fusion(f32[1920,1,256]{2,0,1:T(8,128)S(1)} %convolution_bitcast_fusion, f32[1920,1,256]{2,0,1:T(8,128)S(1)} %convolution_bitcast_fusion.1), kind=kLoop, calls=%fused_computation.7 | loop fusion | flops 983040 | bytes 7864320 | tf_op jit(solution)/shard_map/stack | solution.py:44
  51.0 0.0 reduce-scatter.2.cloned.1.call-update
  51.0 0.0 all-gather.5.cloned.1.call-start
  51.1 51.6 %reduce-scatter.2.cloned.1.call-done = f32[240,2,256]{2,0,1:T(8,128)} async-done(((f32[1920,2,256]{2,0,1:T(8,128)}), f32[240,2,256]{2,0,1:T(8,128)}) %reduce-scatter.2.cloned.1.call-update) | async-done | bytes 491536 | tf_op jit(solution)/shard_map/reduce_scatter | solution.py:43
  102.7 0.0 copy-done.1
  102.7 0.0 copy-done.2
  102.7 2.1 %add_divide_fusion = (f32[240,2,256]{2,0,1:T(8,128)}, f32[240,2,256]{2,0,1:T(8,128)S(1)}, f32[240,2,256]{2,0,1:T(8,128)S(1)}) fusion(f32[240,2,256]{2,0,1:T(8,128)} %reduce-scatter.2.cloned.1.call-done, f32[240,2,256]{2,1,0:T(2,128)S(1)} %copy-done.1, f32[240,2,256]{2,1,0:T(2,128)S(1)} %copy-done.2), kind=kLoop, calls=%fused_computation.18 | loop fusion | flops 1105920 | bytes 2949120 | tf_op jit(solution)/shard_map/div | solution.py:48
  104.8 0.0 all-gather.5.cloned.1.call-update
  104.8 1.2 copy.13
  106.0 1.2 copy.12
  107.1 33.5 %all-gather.5.cloned.1.call-done = f32[1920,2,256]{2,0,1:T(8,128)} async-done(((f32[240,2,256]{2,0,1:T(8,128)}), f32[1920,2,256]{2,0,1:T(8,128)}) %all-gather.5.cloned.1.call-update) | async-done | bytes 3932176 | tf_op jit(solution)/shard_map/all_gather | solution.py:49
  140.7 0.0 copy-done
  140.7 9.1 %bitcast_subtract_fusion = f32[2,1920,512]{2,1,0:T(8,128)} fusion(f32[2,1920,512]{2,1,0:T(8,128)} %param.11, f32[1920,2,256]{2,0,1:T(8,128)} %all-gather.5.cloned.1.call-done, bf16[512,256]{1,0:T(8,128)(2,1)S(1)} %copy-done), kind=kOutput, calls=%fused_computation.6 | convolution fusion | flops 6043729920 | bytes 19922944 | tf_op jit(solution)/shard_map/fwr,dr->wfd/dot_general | solution.py:50
  (4 shorter events, 0.0 us)
Async XLA Ops:
  7.2 36.0 %all-gather.3.cloned.1.call-start = ((), (), s32[]{:S(2)}) async-start(), calls=%async_computation.1 | async-start | bytes 2359296 | tf_op jit(solution)/shard_map/all_gather | solution.py:22
  7.9 94.8 %reduce-scatter.2.cloned.1.call-start = ((), (), s32[]{:S(2)}) async-start(), calls=%async_computation.2 | async-start | bytes 4423680 | tf_op jit(solution)/shard_map/reduce_scatter | solution.py:43
  25.5 8.8 %copy-start.3 = (bf16[64,1920]{1,0:T(8,128)(2,1)S(1)}, bf16[64,1920]{1,0:T(8,128)(2,1)}, u32[]{:S(2)}) copy-start(bf16[64,1920]{1,0:T(8,128)(2,1)} %param.8) | copy-start | bytes 737284
  51.0 51.7 %copy-start.1 = (f32[240,2,256]{2,1,0:T(2,128)S(1)}, f32[240,2,256]{2,1,0:T(2,128)}, u32[]{:S(2)}) copy-start(f32[240,2,256]{2,1,0:T(2,128)} %param.13) | copy-start | bytes 1474564
  51.0 51.7 %copy-start.2 = (f32[240,2,256]{2,1,0:T(2,128)S(1)}, f32[240,2,256]{2,1,0:T(2,128)}, u32[]{:S(2)}) copy-start(f32[240,2,256]{2,1,0:T(2,128)} %param.12) | copy-start | bytes 1474564
  51.0 89.7 %copy-start = (bf16[512,256]{1,0:T(8,128)(2,1)S(1)}, bf16[512,256]{1,0:T(8,128)(2,1)}, u32[]{:S(2)}) copy-start(bf16[512,256]{1,0:T(8,128)(2,1)} %param.10) | copy-start | bytes 786436
  51.0 89.7 %all-gather.5.cloned.1.call-start = ((), (), s32[]{:S(2)}) async-start(), calls=%async_computation.3 | async-start | bytes 4423680 | tf_op jit(solution)/shard_map/all_gather | solution.py:49
Sparse Core Ops, SparseCore 0:
  9.9 30.4 all-gather.2
  51.1 51.5 reduce-scatter.1
  105.2 35.4 all-gather.4
where the time goes:
time: 156 us
  waiting for transfers between devices  85.9 us (55%)
  matrix products  32.3 us (21%)
  blocking collectives  17.6 us (11%)
  between operations  13.8 us (9%)
  other arithmetic  4.27 us (3%)
  local copies, waits for them, and re-layouts  2.33 us (1%)
    reduce_scatter x1, waiting for transfers between devices, on_device(): lax.psum_scatter(jnp.stack([gate_term, up_term], axis=1), 'dp', scatter_d...  51.6 us
    all_gather x1, waiting for transfers between devices, on_device(): direction = lax.all_gather(direction_share, 'dp', axis=0, tiled=True)  33.5 us
    all_gather x1, blocking collectives, on_device(): group_tokens = lax.all_gather(tokens, 'hid', axis=0, tiled=True)  17.6 us
    dot_general x1, matrix products, on_device(): jnp.einsum('fwr,dr->wfd', direction, basis.astype(jnp.float32), precision...  9.06 us
    dot_general x1, matrix products, on_device(): lax.dot_general(group_tokens, weights[1], contract_cols, preferred_elemen...  8.84 us
    dot_general x1, matrix products, on_device(): lax.dot_general(group_tokens, weights[0], contract_cols, preferred_elemen...  8.77 us
  transfers between devices with their start and end apart: 3, of which 2 were waited for; matrix products, arithmetic and copies ran while one was open for 13% of the time, Pallas kernels for 0%

commit v1 on v0

--- a/solution.py
+++ b/solution.py
@@ -7,6 +7,17 @@
 beta_second = 0.95
 step_size = 0.05
 adam_epsilon = 1e-08
+
+
+def around_the_ring(array, mesh_axis, d):
+    peers = lax.axis_size(mesh_axis)
+    route = [(i, (i + 1) % peers) for i in range(peers)]
+    terms = [array]
+    for hop in range(1, peers):
+        terms = [lax.ppermute(terms[0], mesh_axis, route), *terms]
+    whole = jnp.concatenate(terms, axis=d)
+    shift = (lax.axis_index(mesh_axis) + 1) * terms[-1].shape[d]
+    return jnp.roll(whole, shift, axis=d)
 
 
 def silu_pieces(pre_gate):
@@ -46,7 +57,7 @@
     first_new = beta_first * first_moment + (1.0 - beta_first) * gradient
     second_new = beta_second * second_moment + (1.0 - beta_second) * gradient * gradient
     direction_share = first_new / (jnp.sqrt(second_new) + adam_epsilon)
-    direction = lax.all_gather(direction_share, "dp", axis=0, tiled=True)
+    direction = around_the_ring(direction_share, "dp", 0)
     lifted = jnp.einsum("fwr,dr->wfd", direction, basis.astype(jnp.float32), precision=highest)
     master_new = master - step_size * lifted
     return (master_new, first_new, second_new)

time: 156 us -> 189 us (1.21)
  waiting for transfers between devices: 85.9 us -> 115 us
  local copies, waits for them, and re-layouts: 2.33 us -> 9 us
  matrix products: 32.3 us -> 29.3 us
    ppermute x0 -> x7, waiting for transfers between devices: none -> 62.1 us  [around_the_ring(): terms = [lax.ppermute(terms[0], mesh_axis, route), *terms]]
    all_gather x1 -> x0, waiting for transfers between devices: 33.5 us -> none  [on_device(): direction = lax.all_gather(direction_share, 'dp', axis=0, tiled=True)]
    unnamed x10 -> x33, local copies, waits for them, and re-layouts: 2.33 us -> 8.97 us
    dot_general x1, matrix products: 9.06 us -> 6.1 us  [on_device(): jnp.einsum('fwr,dr->wfd', direction, basis.astype(jnp.float32), precision...]
  transfers between devices with their start and end apart: 3 -> 9, of which waited for: 2 -> 8; matrix products, arithmetic and copies ran while one was open for 13% -> 11% of each run, Pallas kernels for 0% -> 0%
where the time goes in v1:
time: 189 us; the launch traced here: 188 us
  waiting for transfers between devices  115 us (61%)
  matrix products  29.3 us (16%)
  blocking collectives  17.6 us (9%)
  between operations  14.3 us (8%)
  local copies, waits for them, and re-layouts  9 us (5%)
  other arithmetic  3.49 us (2%)
    ppermute x7, waiting for transfers between devices, around_the_ring(): terms = [lax.ppermute(terms[0], mesh_axis, route), *terms]  62.1 us
    reduce_scatter x1, waiting for transfers between devices, on_device(): lax.psum_scatter(jnp.stack([gate_term, up_term], axis=1), 'dp', scatter_d...  51.7 us
    all_gather x1, blocking collectives, on_device(): group_tokens = lax.all_gather(tokens, 'hid', axis=0, tiled=True)  17.6 us
    unnamed x33, local copies, waits for them, and re-layouts  8.97 us
    dot_general x1, matrix products, on_device(): lax.dot_general(group_tokens, weights[1], contract_cols, preferred_elemen...  8.84 us
    dot_general x1, matrix products, on_device(): lax.dot_general(group_tokens, weights[0], contract_cols, preferred_elemen...  8.77 us
    dot_general x1, matrix products, on_device(): jnp.einsum('fwr,dr->wfd', direction, basis.astype(jnp.float32), precision...  6.1 us
  transfers between devices with their start and end apart: 9, of which 8 were waited for; matrix products, arithmetic and copies ran while one was open for 11% of the time, Pallas kernels for 0%

profile of v1, /device:TPU:0, one launch (start us, length us, event | category | flops | bytes accessed | tf_op | source)
XLA Modules:
  0.0 188.4 jit_solution(8967825339956676141)
XLA Ops:
  7.9 17.6 %all_gather.6 = bf16[64,4096]{1,0:T(8,128)(2,1)S(1)} all-gather(bf16[16,4096]{1,0:T(8,128)(2,1)} %param.7), channel_id=1, replica_groups=mesh['dp'=8,'hid'=4] {'hid'}, dimensions={0}, use_global_device_ids=true | all-gather | bytes 655360 | tf_op jit(solution)/shard_map/all_gather | solution.py:30
  25.5 8.8 %fusion = f32[64,1920]{1,0:T(8,128)S(1)} fusion(bf16[64,4096]{1,0:T(8,128)(2,1)S(1)} %all_gather.6, bf16[2,1920,4096]{2,1,0:T(8,128)(2,1)} %param.9), kind=kOutput, calls=%fused_computation | convolution fusion | flops 1006632960 | bytes 16744448 | tf_op jit(solution)/shard_map/dot_general | solution.py:37
  34.3 8.8 %fusion.10 = f32[64,1920]{1,0:T(8,128)S(1)} fusion(bf16[64,4096]{1,0:T(8,128)(2,1)S(1)} %all_gather.6, bf16[2,1920,4096]{2,1,0:T(8,128)(2,1)} %param.9, bf16[64,1920]{1,0:T(8,128)(2,1)S(1)} %copy-done.5, f32[64,1920]{1,0:T(8,128)S(1)} %fusion), kind=kOutput, calls=%fused_computation.12 | convolution fusion | flops 1007861760 | bytes 17481728 | tf_op jit(solution)/shard_map/dot_general | solution.py:40
  43.2 2.0 %fusion.22 = f32[64,256]{1,0:T(8,128)S(1)} fusion(bf16[64,4096]{1,0:T(8,128)(2,1)S(1)} %all_gather.6, bf16[4096,256]{1,0:T(8,128)(2,1)} %all-gather.2.cloned.1.call-done), kind=kOutput, calls=%fused_computation.42 | convolution fusion | flops 134217728 | bytes 2686976 | tf_op jit(solution)/shard_map/dot_general | solution.py:31
  45.3 1.8 convolution_bitcast_fusion
  47.1 1.8 convolution_bitcast_fusion.1
  48.8 2.2 %pad_maximum_fusion = f32[1920,2,256]{2,0,1:T(8,128)} fusion(f32[1920,1,256]{2,0,1:T(8,128)S(1)} %convolution_bitcast_fusion, f32[1920,1,256]{2,0,1:T(8,128)S(1)} %convolution_bitcast_fusion.1), kind=kLoop, calls=%fused_computation.7 | loop fusion | flops 983040 | bytes 7864320 | tf_op jit(solution)/shard_map/stack | solution.py:55
  51.0 51.7 %reduce-scatter.2.cloned.1.call-done = f32[240,2,256]{2,0,1:T(8,128)} async-done(((f32[1920,2,256]{2,0,1:T(8,128)}), f32[240,2,256]{2,0,1:T(8,128)}) %reduce-scatter.2.cloned.1.call-update) | async-done | bytes 491536 | tf_op jit(solution)/shard_map/reduce_scatter | solution.py:54
  102.7 1.3 add_divide_fusion
  104.1 9.1 %collective-permute-done = f32[240,2,256]{2,0,1:T(8,128)S(1)} collective-permute-done((f32[240,2,256]{2,0,1:T(8,128)S(1)}, f32[240,2,256]{2,0,1:T(8,128)S(1)}, u32[]{:S(2)}, u32[]{:S(2)}) %collective-permute-start) | collective-permute-done | bytes 491552 | tf_op jit(solution)/shard_map/ppermute | solution.py:17
  113.2 9.2 %collective-permute-done.1 = f32[240,2,256]{2,0,1:T(8,128)S(1)} collective-permute-done((f32[240,2,256]{2,0,1:T(8,128)S(1)}, f32[240,2,256]{2,0,1:T(8,128)S(1)}, u32[]{:S(2)}, u32[]{:S(2)}) %collective-permute-start.1) | collective-permute-done | bytes 491552 | tf_op jit(solution)/shard_map/ppermute | solution.py:17
  122.4 9.2 %collective-permute-done.2 = f32[240,2,256]{2,0,1:T(8,128)S(1)} collective-permute-done((f32[240,2,256]{2,0,1:T(8,128)S(1)}, f32[240,2,256]{2,0,1:T(8,128)S(1)}, u32[]{:S(2)}, u32[]{:S(2)}) %collective-permute-start.2) | collective-permute-done | bytes 491552 | tf_op jit(solution)/shard_map/ppermute | solution.py:17
  131.6 9.2 %collective-permute-done.3 = f32[240,2,256]{2,0,1:T(8,128)S(1)} collective-permute-done((f32[240,2,256]{2,0,1:T(8,128)S(1)}, f32[240,2,256]{2,0,1:T(8,128)S(1)}, u32[]{:S(2)}, u32[]{:S(2)}) %collective-permute-start.3) | collective-permute-done | bytes 491552 | tf_op jit(solution)/shard_map/ppermute | solution.py:17
  140.7 9.2 %collective-permute-done.4 = f32[240,2,256]{2,0,1:T(8,128)S(1)} collective-permute-done((f32[240,2,256]{2,0,1:T(8,128)S(1)}, f32[240,2,256]{2,0,1:T(8,128)S(1)}, u32[]{:S(2)}, u32[]{:S(2)}) %collective-permute-start.4) | collective-permute-done | bytes 491552 | tf_op jit(solution)/shard_map/ppermute | solution.py:17
  150.6 9.3 %collective-permute-done.5 = f32[240,2,256]{2,0,1:T(8,128)} collective-permute-done((f32[240,2,256]{2,0,1:T(8,128)S(1)}, f32[240,2,256]{2,0,1:T(8,128)}, u32[]{:S(2)}, u32[]{:S(2)}) %collective-permute-start.5) | collective-permute-done | bytes 491552 | tf_op jit(solution)/shard_map/ppermute | solution.py:17
  159.9 1.2 copy.12
  161.1 1.2 copy.13
  162.2 7.1 %collective-permute-done.6 = f32[240,2,256]{2,0,1:T(8,128)} collective-permute-done((f32[240,2,256]{2,0,1:T(8,128)}, f32[240,2,256]{2,0,1:T(8,128)}, u32[]{:S(2)}, u32[]{:S(2)}) %collective-permute-start.6) | collective-permute-done | bytes 491552 | tf_op jit(solution)/shard_map/ppermute | solution.py:17
  169.4 1.1 constant_dynamic-update-slice_fusion.15
  170.4 1.1 constant_dynamic-update-slice_fusion.14
  171.5 1.1 constant_dynamic-update-slice_fusion.13
  172.8 1.2 constant_dynamic-update-slice_fusion.7
  174.0 1.1 constant_dynamic-update-slice_fusion.6
  175.4 6.1 %bitcast_subtract_fusion = f32[2,1920,512]{2,1,0:T(8,128)} fusion(f32[2,1920,512]{2,1,0:T(8,128)S(1)} %bitcast.27, f32[3840,2,256]{2,0,1:T(8,128)S(1)} %constant_dynamic-update-slice_fusion, s32[]{:T(128)S(6)} %select_n.14, bf16[512,256]{1,0:T(8,128)(2,1)S(1)} %copy-done.2), kind=kOutput, calls=%fused_computation.6 | convolution fusion | flops 6043729920 | bytes 19922948 | tf_op jit(solution)/shard_map/fwr,dr->wfd/dot_general | solution.py:61
  (40 shorter events, 2.1 us)
Async XLA Ops:
  7.2 36.0 %all-gather.2.cloned.1.call-start = ((), (), s32[]{:S(2)}) async-start(), calls=%async_computation.1 | async-start | bytes 2359296 | tf_op jit(solution)/shard_map/all_gather | solution.py:33
  7.9 94.8 %reduce-scatter.2.cloned.1.call-start = ((), (), s32[]{:S(2)}) async-start(), calls=%async_computation.2 | async-start | bytes 4423680 | tf_op jit(solution)/shard_map/reduce_scatter | solution.py:54
  25.5 8.8 %copy-start.5 = (bf16[64,1920]{1,0:T(8,128)(2,1)S(1)}, bf16[64,1920]{1,0:T(8,128)(2,1)}, u32[]{:S(2)}) copy-start(bf16[64,1920]{1,0:T(8,128)(2,1)} %param.8) | copy-start | bytes 737284
  45.3 57.5 %copy-start.3 = (f32[240,2,256]{2,1,0:T(2,128)S(1)}, f32[240,2,256]{2,1,0:T(2,128)}, u32[]{:S(2)}) copy-start(f32[240,2,256]{2,1,0:T(2,128)} %param.13) | copy-start | bytes 1474564
  45.3 57.5 %copy-start.4 = (f32[240,2,256]{2,1,0:T(2,128)S(1)}, f32[240,2,256]{2,1,0:T(2,128)}, u32[]{:S(2)}) copy-start(f32[240,2,256]{2,1,0:T(2,128)} %param.12) | copy-start | bytes 1474564
  104.0 9.2 %collective-permute-start = (f32[240,2,256]{2,0,1:T(8,128)S(1)}, f32[240,2,256]{2,0,1:T(8,128)S(1)}, u32[]{:S(2)}, u32[]{:S(2)}) collective-permute-start(f32[240,2,256]{2,0,1:T(8,128)S(1)} %get-tuple-element.6), channel_id=1, source_target_pairs={{0,4},{4,8},{8,12},{12,16},{16,20},{20,24},{24,28},{28,0},{1,5},{5... | collective-permute-start | bytes 1474568 | tf_op jit(solution)/shard_map/ppermute | solution.py:17
  113.2 9.2 %collective-permute-start.1 = (f32[240,2,256]{2,0,1:T(8,128)S(1)}, f32[240,2,256]{2,0,1:T(8,128)S(1)}, u32[]{:S(2)}, u32[]{:S(2)}) collective-permute-start(f32[240,2,256]{2,0,1:T(8,128)S(1)} %collective-permute-done), channel_id=1, source_target_pairs={{0,4},{4,8},{8,12},{12,16},{16,20},{20,24},{24,28},{28,0},{1,5},{5... | collective-permute-start | bytes 1474568 | tf_op jit(solution)/shard_map/ppermute | solution.py:17
  122.4 9.2 %collective-permute-start.2 = (f32[240,2,256]{2,0,1:T(8,128)S(1)}, f32[240,2,256]{2,0,1:T(8,128)S(1)}, u32[]{:S(2)}, u32[]{:S(2)}) collective-permute-start(f32[240,2,256]{2,0,1:T(8,128)S(1)} %collective-permute-done.1), channel_id=1, source_target_pairs={{0,4},{4,8},{8,12},{12,16},{16,20},{20,24},{24,28},{28,0},{1,5},{5... | collective-permute-start | bytes 1474568 | tf_op jit(solution)/shard_map/ppermute | solution.py:17
  131.6 9.2 %collective-permute-start.3 = (f32[240,2,256]{2,0,1:T(8,128)S(1)}, f32[240,2,256]{2,0,1:T(8,128)S(1)}, u32[]{:S(2)}, u32[]{:S(2)}) collective-permute-start(f32[240,2,256]{2,0,1:T(8,128)S(1)} %collective-permute-done.2), channel_id=1, source_target_pairs={{0,4},{4,8},{8,12},{12,16},{16,20},{20,24},{24,28},{28,0},{1,5},{5... | collective-permute-start | bytes 1474568 | tf_op jit(solution)/shard_map/ppermute | solution.py:17
  140.7 9.2 %collective-permute-start.4 = (f32[240,2,256]{2,0,1:T(8,128)S(1)}, f32[240,2,256]{2,0,1:T(8,128)S(1)}, u32[]{:S(2)}, u32[]{:S(2)}) collective-permute-start(f32[240,2,256]{2,0,1:T(8,128)S(1)} %collective-permute-done.3), channel_id=1, source_target_pairs={{0,4},{4,8},{8,12},{12,16},{16,20},{20,24},{24,28},{28,0},{1,5},{5... | collective-permute-start | bytes 1474568 | tf_op jit(solution)/shard_map/ppermute | solution.py:17
  149.9 0.8 copy-start
  150.6 9.3 %collective-permute-start.5 = (f32[240,2,256]{2,0,1:T(8,128)S(1)}, f32[240,2,256]{2,0,1:T(8,128)}, u32[]{:S(2)}, u32[]{:S(2)}) collective-permute-start(f32[240,2,256]{2,0,1:T(8,128)S(1)} %collective-permute-done.4), channel_id=1, source_target_pairs={{0,4},{4,8},{8,12},{12,16},{16,20},{20,24},{24,28},{28,0},{1,5},{5... | collective-permute-start | bytes 1474568 | tf_op jit(solution)/shard_map/ppermute | solution.py:17
  159.9 9.5 %collective-permute-start.6 = (f32[240,2,256]{2,0,1:T(8,128)}, f32[240,2,256]{2,0,1:T(8,128)}, u32[]{:S(2)}, u32[]{:S(2)}) collective-permute-start(f32[240,2,256]{2,0,1:T(8,128)} %collective-permute-done.5), channel_id=1, source_target_pairs={{0,4},{4,8},{8,12},{12,16},{16,20},{20,24},{24,28},{28,0},{1,5},{5... | collective-permute-start | bytes 1474568 | tf_op jit(solution)/shard_map/ppermute | solution.py:17
  159.9 15.2 %copy-start.1 = (f32[240,2,256]{2,0,1:T(8,128)S(1)}, f32[240,2,256]{2,0,1:T(8,128)}, u32[]{:S(2)}) copy-start(f32[240,2,256]{2,0,1:T(8,128)} %copy-done) | copy-start | bytes 1474564
  162.2 13.2 %slice-start = ((s8[7864320]{0:T(1024)(128)(4,1)}), s8[4194304]{0:T(1024)(128)(4,1)S(1)}, s32[]{:S(2)}) async-start(s8[7864320]{0:T(1024)(128)(4,1)} %bitcast.26), calls=%async_computation.3 | async-start | bytes 8388608
  162.2 13.2 %copy-start.2 = (bf16[512,256]{1,0:T(8,128)(2,1)S(1)}, bf16[512,256]{1,0:T(8,128)(2,1)}, u32[]{:S(2)}) copy-start(bf16[512,256]{1,0:T(8,128)(2,1)} %param.10) | copy-start | bytes 786436
  172.8 2.6 %slice-start.1 = ((s8[7864320]{0:T(1024)(128)(4,1)}), s8[3670016]{0:T(1024)(128)(4,1)S(1)}, s32[]{:S(2)}) async-start(s8[7864320]{0:T(1024)(128)(4,1)} %bitcast.26), calls=%async_computation.4 | async-start | bytes 7340032
Sparse Core Ops, SparseCore 0:
  9.9 30.4 all-gather.1
  51.1 51.5 reduce-scatter.1
